TPU v7x, 32 devices: a whole 2x2x4 slice. The times are simulated.
32 devices in a mesh: group: 4 (over x, core), member: 8 (over z, y).
Axes of the slice: x: 2, y: 2, z: 4, core: 2. Of those that a mesh axis runs over, the one named last changes fastest.
Arguments:
- right_side: float32 [32, 256, 4096], P(None, 'group', 'member'), may hold values from -8 to 8
- diagonal: float32 [256, 4096], P('group', 'member'), may hold values from 0.02 to 1
- face_weight: float32 [2, 256, 4096], P(None, 'group', 'member'), may hold values from 0.5 to 2
- aggregation: int32 [256, 4096], P('group', 'member'), may hold values from 0 to 127, as said below
Outputs:
- solution_field: float32 [32, 256, 4096], P(None, 'group', 'member')
Inputs may be any that keep to these rules, and one draw needn't show every extreme that they name: `aggregation`: each cell names one aggregate of its own device block; the aggregates are irregular patches.
All inputs are finite; a program needn't handle non-finite values.
Results may differ from a plain program's by a relative error of at most 0.0003.
Values sent between devices are 32-bit elements; how exact they have to be, the bound alone decides.
A program may use at most 128 MiB of HBM per device.

v0:
```python
import functools

import jax
import jax.numpy as jnp
from jax import lax
from jax.experimental import pallas as pl
from jax.experimental.pallas import tpu as pltpu
from jax.sharding import PartitionSpec as P

AGG = 128
POST = 2
CHEB = 6
OMEGA = 0.8
RATIO = 30.0
LANES = 128
MESH = pl.DeviceIdType.MESH
F32 = jnp.float32
BF16 = jnp.bfloat16
NT = (((1,), (1,)), ((), ()))


def passed_along(value, axis, steps):
    count = lax.axis_size(axis)
    initial, last = (max(0, -steps), min(count, count - steps))
    return lax.ppermute(value, axis, [(source, source + steps) for source in range(initial, last)])


def split(value):
    high = value.astype(BF16)
    return high, (value - high.astype(F32)).astype(BF16)


def coarse_kernel(rows, cell_ref, edge_ref, w_ref, acc):
    step = pl.program_id(0)

    @pl.when(step == 0)
    def _():
        acc[...] = jnp.zeros_like(acc)

    width = cell_ref.shape[2]
    label = lax.broadcasted_iota(jnp.int32, (AGG, width), 0).astype(F32)
    total = jnp.zeros(acc.shape, F32)
    for x in range(rows):
        cell = cell_ref[x]
        own = label == cell[0:1]
        hot = jnp.where(own, 1.0, 0.0).astype(BF16)
        value = jnp.where(own, cell[3:4], 0.0)
        value = value - jnp.where(label == cell[1:2], cell[4:5], 0.0)
        value = value - jnp.where(label == cell[2:3], cell[5:6], 0.0)
        high, low = split(value)
        both = jnp.concatenate([high, low], axis=0)
        total = total + lax.dot_general(hot, both, NT, preferred_element_type=F32)
    acc[...] += total

    @pl.when(step == pl.num_programs(0) - 1)
    def _():
        half = acc[:, :AGG] + acc[:, AGG:]
        w_ref[0:AGG] = half + half.T
        edge = edge_ref[...]
        lab = lax.broadcasted_iota(jnp.int32, (AGG, LANES), 0).astype(F32)

        def lower(first, second, weight):
            left = jnp.where(lab == edge[first:first + 1], edge[weight:weight + 1], 0.0)
            right = jnp.where(lab == edge[second:second + 1], 1.0, 0.0)
            return -lax.dot_general(
                left, right, NT, precision=lax.Precision.HIGHEST, preferred_element_type=F32
            )

        w_ref[AGG:2 * AGG] = lower(0, 1, 2)
        w_ref[2 * AGG:3 * AGG] = lower(4, 3, 5)


def cycle_kernel(
    n_group, n_member, rhs_ref, coef_ref, w_ref, out_ref,
    b, f, g, h, col_send, col_recv, dir_send, dir_recv, lm_send, lm_recv,
    halo_ssem, halo_rsem, dir_ssem, dir_rsem, lm_ssem, lm_rsem,
):
    rows, n_rhs, width = rhs_ref.shape
    tiles = width // LANES
    gi = lax.axis_index("group")
    mi = lax.axis_index("member")
    g_up, g_down = lax.rem(gi + 1, n_group), lax.rem(gi + n_group - 1, n_group)
    m_up, m_down = lax.rem(mi + 1, n_member), lax.rem(mi + n_member - 1, n_member)

    barrier = pltpu.get_barrier_semaphore()
    for peer in (g_up, g_down):
        pl.semaphore_signal(barrier, inc=1, device_id=(peer, mi), device_id_type=MESH)
    for off in range(1, n_member):
        peer = lax.rem(mi + off, n_member)
        pl.semaphore_signal(barrier, inc=1, device_id=(gi, peer), device_id_type=MESH)

    lane = lax.broadcasted_iota(jnp.int32, (n_rhs, LANES), 1)
    label = lax.broadcasted_iota(jnp.int32, (AGG, width), 0).astype(F32)

    def remote(src, dst, ssem, rsem, target):
        return pltpu.make_async_remote_copy(
            src_ref=src, dst_ref=dst, send_sem=ssem, recv_sem=rsem,
            device_id=target, device_id_type=MESH,
        )

    def exchange(phase, buf):
        plan = (
            (buf.at[rows], buf.at[0], (g_up, mi)),
            (buf.at[1], buf.at[rows + 1], (g_down, mi)),
            (col_send.at[phase, 0], col_recv.at[phase, 0], (gi, m_up)),
            (col_send.at[phase, 1], col_recv.at[phase, 1], (gi, m_down)),
        )
        copies = [
            remote(s, d, halo_ssem.at[phase, i], halo_rsem.at[phase, i], t)
            for i, (s, d, t) in enumerate(plan)
        ]
        for copy in copies:
            copy.start()
        return copies

    def finish(copies):
        for copy in copies:
            copy.wait()

    def pack(x, value, carry):
        last, first = carry
        last = jnp.where(lane == x + 1, pltpu.roll(value[:, width - LANES:], x + 2, 1), last)
        first = jnp.where(lane == x, pltpu.roll(value[:, :LANES], x, 1), first)
        return last, first

    def store_columns(phase, carry):
        col_send[phase, 0] = carry[0]
        col_send[phase, 1] = carry[1]

    empty = (jnp.zeros((n_rhs, LANES), F32), jnp.zeros((n_rhs, LANES), F32))

    def neighbours(phase, buf, x, coef):
        cur = buf[x + 1]
        prev_t = pltpu.roll(col_recv[phase, 0], 127 - x, 1)
        back_t = pltpu.roll(col_recv[phase, 1], 127 - x, 1)
        parts = [cur[:, k * LANES:(k + 1) * LANES] for k in range(tiles)]
        right = [prev_t] + [pltpu.roll(p, 1, 1) for p in parts]
        left = [pltpu.roll(p, LANES - 1, 1) for p in parts] + [back_t]
        low = [jnp.where(lane == 0, right[k], right[k + 1]) for k in range(tiles)]
        high = [jnp.where(lane == LANES - 1, left[k + 1], left[k]) for k in range(tiles)]
        low = jnp.concatenate(low, axis=1)
        high = jnp.concatenate(high, axis=1)
        total = coef[0:1] * buf[x + 2] + coef[1:2] * buf[x]
        return cur, total + coef[2:3] * high + coef[3:4] * low

    def hot_of(coef):
        return jnp.where(label == coef[6:7], 1.0, 0.0).astype(BF16)

    def scale(x, carry):
        value = rhs_ref[x] * coef_ref[x][4:5]
        b[x + 1] = value
        return pack(x, value, carry)

    store_columns(0, lax.fori_loop(0, rows, scale, empty, unroll=2))
    w = w_ref[...]
    lm = jnp.sum(jnp.abs(w), axis=0, keepdims=True)
    lm_send[...] = jnp.broadcast_to(lm, lm_send.shape)
    pl.semaphore_wait(barrier, n_member + 1)

    first = exchange(0, b)
    lm_copies = []
    for off in range(1, n_member):
        peer = lax.rem(mi + off, n_member)
        copy = remote(
            lm_send, lm_recv.at[off - 1], lm_ssem.at[off - 1], lm_rsem.at[off - 1], (gi, peer)
        )
        copy.start()
        lm_copies.append(copy)
    w_high, w_low = split(w)
    finish(first)

    def pre(x, carry):
        cur, total = neighbours(0, b, x, coef_ref[x])
        value = (2.0 - OMEGA) * cur + total
        f[x + 1] = value
        return pack(x, value, carry)

    store_columns(1, lax.fori_loop(0, rows, pre, empty, unroll=2))
    finish(exchange(1, f))

    def restrict(x, carry):
        coef = coef_ref[x]
        cur, total = neighbours(1, f, x, coef)
        resid = (b[x + 1] - OMEGA * cur + total) * coef[5:6]
        high, low = split(resid)
        both = jnp.concatenate([high, low], axis=0)
        return carry + lax.dot_general(both, hot_of(coef), NT, preferred_element_type=F32)

    sums = lax.fori_loop(0, rows, restrict, jnp.zeros((2 * n_rhs, AGG), F32), unroll=4)
    resid = sums[:n_rhs] + sums[n_rhs:]

    for copy in lm_copies:
        copy.wait()
    lm8 = lm_send[...]
    for off in range(1, n_member):
        lm8 = jnp.maximum(lm8, lm_recv[off - 1])
    lmax = jnp.max(lm8[0:1], axis=1, keepdims=True)
    lmin = lmax / RATIO
    theta = (lmax + lmin) / 2.0
    delta = (lmax - lmin) / 2.0
    sigma = theta / delta
    rho = 1.0 / sigma
    direc = resid / theta
    sol = jnp.zeros_like(resid)
    for step in range(CHEB):
        if step + 1 < CHEB:
            dir_send[step] = direc
            copies = [
                remote(
                    dir_send.at[step], dir_recv.at[step, i],
                    dir_ssem.at[step, i], dir_rsem.at[step, i], (gi, peer),
                )
                for i, peer in enumerate((m_up, m_down))
            ]
            for copy in copies:
                copy.start()
            sol = sol + direc
            rho_new = 1.0 / (2.0 * sigma - rho)
            finish(copies)
            vec = jnp.concatenate([direc, dir_recv[step, 0], dir_recv[step, 1]], axis=1)
            v_high, v_low = split(vec)
            both = jnp.concatenate([v_high, v_low], axis=0)
            prod = jnp.dot(both, w_high, preferred_element_type=F32)
            prod = prod[:n_rhs] + prod[n_rhs:]
            prod = prod + jnp.dot(v_high, w_low, preferred_element_type=F32)
            resid = resid - prod
            direc = rho_new * rho * direc + (2.0 * rho_new / delta) * resid
            rho = rho_new
        else:
            sol = sol + direc

    e_high, e_low = split(sol)
    e_both = jnp.concatenate([e_high, e_low], axis=0)

    def prolong(x, carry):
        spread = jnp.dot(e_both, hot_of(coef_ref[x]), preferred_element_type=F32)
        value = f[x + 1] + spread[:n_rhs] + spread[n_rhs:]
        g[x + 1] = value
        return pack(x, value, carry)

    store_columns(2, lax.fori_loop(0, rows, prolong, empty, unroll=4))
    finish(exchange(2, g))

    def post(x, carry):
        cur, total = neighbours(2, g, x, coef_ref[x])
        value = b[x + 1] + (1.0 - OMEGA) * cur + total
        h[x + 1] = value
        return pack(x, value, carry)

    store_columns(3, lax.fori_loop(0, rows, post, empty, unroll=2))
    finish(exchange(3, h))

    def final(x, carry):
        cur, total = neighbours(3, h, x, coef_ref[x])
        out_ref[x] = b[x + 1] + (1.0 - OMEGA) * cur + total
        return carry

    lax.fori_loop(0, rows, final, 0, unroll=2)


def local(right_side, diagonal, face_weight, aggregation):
    n_group, n_member = lax.axis_size("group"), lax.axis_size("member")
    n_rhs, rows, width = right_side.shape
    wx = face_weight[0]
    wy = face_weight[1]
    agg = aggregation.astype(F32)
    low_row = passed_along(wx[-1:, :], "group", 1)
    forward = passed_along(jnp.stack([agg[:, -1] + 1.0, wy[:, -1]]), "member", 1)
    backward = passed_along(agg[:, 0] + 1.0, "member", -1)
    below_weight = forward[1]
    wx_low = jnp.concatenate([low_row, wx[:-1, :]], axis=0)
    wy_low = jnp.concatenate([below_weight[:, None], wy[:, :-1]], axis=1)
    diagf = diagonal + wx + wy + wx_low + wy_low
    xs = lax.broadcasted_iota(jnp.int32, (rows, width), 0)
    ys = lax.broadcasted_iota(jnp.int32, (rows, width), 1)
    last_x = (lax.axis_index("group") == n_group - 1) & (xs == rows - 1)
    last_y = (lax.axis_index("member") == n_member - 1) & (ys == width - 1)
    q = OMEGA / diagf
    coef = jnp.stack(
        [
            jnp.where(last_x, 0.0, q * wx), q * wx_low, jnp.where(last_y, 0.0, q * wy), q * wy_low,
            q, diagf * (1.0 / OMEGA), agg, agg,
        ],
        axis=1,
    )
    agg_x = jnp.concatenate([agg[1:], agg[-1:]], axis=0)
    agg_y = jnp.concatenate([agg[:, 1:], agg[:, -1:]], axis=1)
    cell = jnp.stack(
        [
            agg, agg_x, agg_y, 0.5 * diagf,
            jnp.where(xs == rows - 1, 0.0, wx), jnp.where(ys == width - 1, 0.0, wy), agg, agg,
        ],
        axis=1,
    )
    edge = jnp.stack(
        [
            forward[0] - 1.0, agg[:, 0], below_weight, agg[:, -1], backward - 1.0, wy[:, -1],
            below_weight, below_weight,
        ]
    )
    edge = jnp.pad(edge, ((0, 0), (0, LANES - rows)), constant_values=-1.0)

    block = 8
    w = pl.pallas_call(
        functools.partial(coarse_kernel, block),
        grid=(rows // block,),
        out_shape=jax.ShapeDtypeStruct((3 * AGG, AGG), F32),
        in_specs=[
            pl.BlockSpec((block, 8, width), lambda i: (i, 0, 0)),
            pl.BlockSpec((8, LANES), lambda i: (0, 0)),
        ],
        out_specs=pl.BlockSpec((3 * AGG, AGG), lambda i: (0, 0)),
        scratch_shapes=[pltpu.VMEM((AGG, 2 * AGG), F32)],
    )(cell, edge)

    padded = pltpu.VMEM((rows + 2, n_rhs, width), F32)
    dma = pltpu.SemaphoreType.DMA
    vmem = pl.BlockSpec(memory_space=pltpu.VMEM)
    out = pl.pallas_call(
        functools.partial(cycle_kernel, n_group, n_member),
        out_shape=jax.ShapeDtypeStruct((rows, n_rhs, width), F32),
        in_specs=[vmem] * 3,
        out_specs=vmem,
        scratch_shapes=[
            padded, padded, padded, padded,
            pltpu.VMEM((4, 2, n_rhs, LANES), F32),
            pltpu.VMEM((4, 2, n_rhs, LANES), F32),
            pltpu.VMEM((CHEB - 1, n_rhs, AGG), F32),
            pltpu.VMEM((CHEB - 1, 2, n_rhs, AGG), F32),
            pltpu.VMEM((8, AGG), F32),
            pltpu.VMEM((n_member - 1, 8, AGG), F32),
            dma((4, 4)), dma((4, 4)),
            dma((CHEB - 1, 2)), dma((CHEB - 1, 2)),
            dma((n_member - 1,)), dma((n_member - 1,)),
        ],
        compiler_params=pltpu.CompilerParams(
            collective_id=0, has_side_effects=True, vmem_limit_bytes=48 * 1024 * 1024
        ),
    )(right_side.transpose(1, 0, 2), coef, w)
    return out.transpose(1, 0, 2)


def solution(mesh):
    placed = (
        P(None, "group", "member"),
        P("group", "member"),
        P(None, "group", "member"),
        P("group", "member"),
    )
    return jax.shard_map(
        local, mesh=mesh, in_specs=placed, out_specs=P(None, "group", "member"), check_vma=False
    )
```

profile of v0, /device:TPU:0, one launch (start us, length us, event | category | flops | bytes accessed | tf_op | source)
XLA Modules:
  0.0 118.1 jit_solution(14642561382721539151)
XLA Ops:
  0.0 0.7 slice_bitcast_fusion.1
  0.7 2.3 %collective-permute-start = (f32[1,512]{1,0:T(1,128)S(1)}, f32[1,512]{1,0:T(1,128)S(1)}, u32[]{:S(2)}, u32[]{:S(2)}) collective-permute-start(f32[1,512]{1,0:T(1,128)S(1)} %slice_bitcast_fusion.1), channel_id=1, source_target_pairs={{0,8},{8,16},{16,24},{1,9},{9,17},{17,25},{2,10},{10,18},{18,26},{... | collective-permute-start | bytes 6152 | tf_op jit(solution)/shard_map/ppermute | solution.py:25
  3.1 0.9 convert_element_type.3
  4.0 0.2 add_reduce_fusion
  4.2 1.3 %collective-permute-start.2 = (f32[64]{0:T(128)S(1)}, f32[64]{0:T(128)S(1)}, u32[]{:S(2)}, u32[]{:S(2)}) collective-permute-start(f32[64]{0:T(128)S(1)} %get-tuple-element.5), channel_id=1, source_target_pairs={{1,0},{2,1},{3,2},{4,3},{5,4},{6,5},{7,6},{9,8},{10,9},{11,10},{12... | collective-permute-start | bytes 776 | tf_op jit(solution)/shard_map/ppermute | solution.py:25
  5.5 0.9 fusion.7
  6.4 0.2 slice_reduce_fusion
  6.6 4.9 %collective-permute-start.1 = (f32[2,64]{1,0:T(2,128)S(1)}, f32[2,64]{1,0:T(2,128)S(1)}, u32[]{:S(2)}, u32[]{:S(2)}) collective-permute-start(f32[2,64]{1,0:T(2,128)S(1)} %pad_maximum_fusion.3), channel_id=1, source_target_pairs={{0,1},{1,2},{2,3},{3,4},{4,5},{5,6},{6,7},{8,9},{9,10},{10,11},{11... | collective-permute-start | bytes 1544 | tf_op jit(solution)/shard_map/ppermute | solution.py:25
  11.5 0.1 stack.60
  11.6 0.9 slice_bitcast_fusion
  12.6 0.1 slice.71
  12.7 1.0 bitcast_select_fusion
  13.7 0.1 pad_maximum_fusion.2
  13.8 0.1 broadcast_select_fusion
  14.0 0.1 copy.31
  14.1 0.1 stack.63
  14.2 0.1 copy.29
  14.3 0.0 copy-start.1
  14.4 0.0 copy-start.2
  14.4 6.7 %copy.39 = f32[32,64,512]{2,0,1:T(8,128)} copy(f32[32,64,512]{2,1,0:T(8,128)} %param.4) | data formatting | bytes 8388608 | tf_op args[0]
  21.0 0.0 collective-permute-done.2
  21.1 0.0 collective-permute-done.1
  21.1 0.1 copy.21
  21.2 0.6 pad.4.edge_ref
  21.8 0.0 collective-permute-done
  21.8 0.0 copy-done.1
  21.8 0.0 copy-done.2
  21.8 0.1 multiply_bitcast_fusion
  21.9 0.1 copy.30
  22.1 0.1 select_bitcast_fusion
  22.2 0.1 copy.24
  22.3 0.1 copy.22
  22.5 0.1 copy.27
  22.6 0.1 copy.26
  22.8 0.1 copy.25
  22.9 0.1 copy.23
  23.1 2.6 %stack.65.cell_ref = f32[64,8,512]{2,1,0:T(8,128)} concatenate(f32[64,1,512]{2,1,0:T(1,128)S(1)} %stack.60, f32[64,1,512]{2,1,0:T(1,128)S(1)} %copy.29, f32[64,1,512]{2,1,0:T(1,128)S(1)} %stack.63, f32[64,1,512]{2,1,0:T(1,128)S(1)} %copy.30, f32[64,1,512]{2,1,0:T(1,128)S(1)} %copy.31, f32[64,1,512]{2,1,0:T(1,128)S(1)} %broadcast_select_fusion, f32[64,1,512]{2,1,0:T(1,128)S(1)} %stack.60, ...), dimensions={1} | concatenate | bytes 2097152 | tf_op jit(solution)/shard_map/stack | solution.py:288
  25.6 11.0 %shard_map.46.w_ref = f32[384,128]{1,0:T(8,128)} custom-call(f32[64,8,512]{2,1,0:T(8,128)} %stack.65.cell_ref, f32[8,128]{1,0:T(8,128)} %pad.4.edge_ref), custom_call_target="tpu_custom_call" | custom-call | tf_op jit(solution)/shard_map/pallas_call | solution.py:304
  36.6 1.6 %stack.61.coef_ref = f32[64,8,512]{2,1,0:T(8,128)S(1)} concatenate(f32[64,1,512]{2,1,0:T(1,128)S(1)} %copy.22, f32[64,1,512]{2,1,0:T(1,128)S(1)} %copy.23, f32[64,1,512]{2,1,0:T(1,128)S(1)} %copy.24, f32[64,1,512]{2,1,0:T(1,128)S(1)} %copy.25, f32[64,1,512]{2,1,0:T(1,128)S(1)} %copy.26, f32[64,1,512]{2,1,0:T(1,128)S(1)} %copy.27, f32[64,1,512]{2,1,0:T(1,128)S(1)} %stack.60, ...), dimensions={1} | concatenate | bytes 2097152 | tf_op jit(solution)/shard_map/stack | solution.py:279
  38.3 0.0 copy-start
  38.3 0.9 copy-done
  39.2 74.5 %shard_map.47 = f32[64,32,512]{2,1,0:T(8,128)S(1)} custom-call(f32[64,32,512]{2,1,0:T(8,128)} %bitcast.60, f32[64,8,512]{2,1,0:T(8,128)S(1)} %stack.61.coef_ref, f32[384,128]{1,0:T(8,128)S(1)} %copy-done), custom_call_target="tpu_custom_call" | custom-call | tf_op jit(solution)/shard_map/pallas_call | solution.py:319
  113.7 4.4 %copy.32 = f32[32,64,512]{2,1,0:T(8,128)} copy(f32[32,64,512]{2,0,1:T(8,128)S(1)} %bitcast.59) | data formatting | bytes 8388608 | tf_op jit(solution)/shard_map/transpose | solution.py:340
  (12 shorter events, 0.1 us)
Async XLA Ops:
  0.7 21.1 %collective-permute-start = (f32[1,512]{1,0:T(1,128)S(1)}, f32[1,512]{1,0:T(1,128)S(1)}, u32[]{:S(2)}, u32[]{:S(2)}) collective-permute-start(f32[1,512]{1,0:T(1,128)S(1)} %slice_bitcast_fusion.1), channel_id=1, source_target_pairs={{0,8},{8,16},{16,24},{1,9},{9,17},{17,25},{2,10},{10,18},{18,26},{... | collective-permute-start | bytes 6152 | tf_op jit(solution)/shard_map/ppermute | solution.py:25
  4.2 16.9 %collective-permute-start.2 = (f32[64]{0:T(128)S(1)}, f32[64]{0:T(128)S(1)}, u32[]{:S(2)}, u32[]{:S(2)}) collective-permute-start(f32[64]{0:T(128)S(1)} %get-tuple-element.5), channel_id=1, source_target_pairs={{1,0},{2,1},{3,2},{4,3},{5,4},{6,5},{7,6},{9,8},{10,9},{11,10},{12... | collective-permute-start | bytes 776 | tf_op jit(solution)/shard_map/ppermute | solution.py:25
  6.6 14.4 %collective-permute-start.1 = (f32[2,64]{1,0:T(2,128)S(1)}, f32[2,64]{1,0:T(2,128)S(1)}, u32[]{:S(2)}, u32[]{:S(2)}) collective-permute-start(f32[2,64]{1,0:T(2,128)S(1)} %pad_maximum_fusion.3), channel_id=1, source_target_pairs={{0,1},{1,2},{2,3},{3,4},{4,5},{5,6},{6,7},{8,9},{9,10},{10,11},{11... | collective-permute-start | bytes 1544 | tf_op jit(solution)/shard_map/ppermute | solution.py:25
  14.3 7.5 %copy-start.1 = (f32[2,64,512]{2,1,0:T(8,128)S(1)}, f32[2,64,512]{2,1,0:T(8,128)}, u32[]{:S(2)}) copy-start(f32[2,64,512]{2,1,0:T(8,128)} %param.6) | copy-start | bytes 786436
  14.4 7.4 %copy-start.2 = (f32[64,512]{1,0:T(8,128)S(1)}, f32[64,512]{1,0:T(8,128)}, u32[]{:S(2)}) copy-start(f32[64,512]{1,0:T(8,128)} %param.5) | copy-start | bytes 393220
  38.3 0.9 copy-start
where the time goes:
time: 119 us; the launch traced here: 118 us
  Pallas kernels  85.5 us (72%)
  local copies, waits for them, and re-layouts  21.2 us (18%)
  starting transfers between devices  8.52 us (7%)
  other arithmetic  2.6 us (2%)
    pallas_call x1, Pallas kernels, local(): pl.pallas_call(functools.partial(cycle_kernel, n_group, n_member), out_sh...  74.5 us
    pallas_call x1, Pallas kernels, local(): pl.pallas_call(functools.partial(coarse_kernel, block), grid=(rows // blo...  11 us
    ppermute x3, starting transfers between devices, passed_along(): lax.ppermute(value, axis, [(source, source + steps) for source in range(i...  8.52 us
    unnamed x7, local copies, waits for them, and re-layouts  7.61 us
    transpose x1, local copies, waits for them, and re-layouts, local(): return out.transpose(1, 0, 2)  4.44 us
    another operation x4, local copies, waits for them, and re-layouts, local(): jnp.stack([agg, agg_x, agg_y, 0.5 * diagf, jnp.where(xs == rows - 1, 0.0,...  2.92 us
    another operation x8, local copies, waits for them, and re-layouts, local(): jnp.stack([jnp.where(last_x, 0.0, q * wx), q * wx_low, jnp.where(last_y,...  2.52 us
  transfers between devices with their start and end apart: 3, of which 0 were waited for; matrix products, arithmetic and copies ran while one was open for 10% of the time, Pallas kernels for 0%

commit v1 on v0

v1 whole, which is shorter than its diff:
```python
import functools

import jax
import jax.numpy as jnp
from jax import lax
from jax.experimental import pallas as pl
from jax.experimental.pallas import tpu as pltpu
from jax.sharding import PartitionSpec as P

AGG = 128
POST = 2
CHEB = 6
OMEGA = 0.8
RATIO = 30.0
LANES = 128
MESH = pl.DeviceIdType.MESH
F32 = jnp.float32
BF16 = jnp.bfloat16
NT = (((1,), (1,)), ((), ()))


def split(value):
    high = value.astype(BF16)
    return high, (value - high.astype(F32)).astype(BF16)


AX, AX_LOW, AY, AY_LOW, Q, Q_INV, LABEL, LABEL_X, LABEL_Y, WX, WY, HALF = range(12)
D_BLOCK = 4


def cycle_kernel(
    n_group, n_member, rhs_hbm, diag_ref, face_ref, agg_ref, out_ref,
    rhs, cf, acc, low_row_ref, below_w_ref, below_a_ref, above_a_ref,
    b, f, g, h, col_send, col_recv, dir_send, dir_recv, lm_send, lm_recv,
    rhs_sem, edge_ssem, edge_rsem, halo_ssem, halo_rsem, dir_ssem, dir_rsem, lm_ssem, lm_rsem,
):
    rows, n_rhs, width = rhs.shape
    tiles = width // LANES
    gi = lax.axis_index("group")
    mi = lax.axis_index("member")
    g_up, g_down = lax.rem(gi + 1, n_group), lax.rem(gi + n_group - 1, n_group)
    m_up, m_down = lax.rem(mi + 1, n_member), lax.rem(mi + n_member - 1, n_member)

    def fetch(x):
        return pltpu.make_async_copy(rhs_hbm.at[:, x, :], rhs.at[x], rhs_sem.at[x])

    def start_fetch(x, carry):
        fetch(x).start()
        return carry

    lax.fori_loop(0, rows, start_fetch, 0)

    barrier = pltpu.get_barrier_semaphore()
    for peer in (g_up, g_down):
        pl.semaphore_signal(barrier, inc=1, device_id=(peer, mi), device_id_type=MESH)
    for off in range(1, n_member):
        peer = lax.rem(mi + off, n_member)
        pl.semaphore_signal(barrier, inc=1, device_id=(gi, peer), device_id_type=MESH)

    lane = lax.broadcasted_iota(jnp.int32, (n_rhs, LANES), 1)
    label = lax.broadcasted_iota(jnp.int32, (AGG, width), 0).astype(F32)

    def remote(src, dst, ssem, rsem, target):
        return pltpu.make_async_remote_copy(
            src_ref=src, dst_ref=dst, send_sem=ssem, recv_sem=rsem,
            device_id=target, device_id_type=MESH,
        )

    def exchange(phase, buf):
        plan = (
            (buf.at[rows], buf.at[0], (g_up, mi)),
            (buf.at[1], buf.at[rows + 1], (g_down, mi)),
            (col_send.at[phase, 0], col_recv.at[phase, 0], (gi, m_up)),
            (col_send.at[phase, 1], col_recv.at[phase, 1], (gi, m_down)),
        )
        copies = [
            remote(s, d, halo_ssem.at[phase, i], halo_rsem.at[phase, i], t)
            for i, (s, d, t) in enumerate(plan)
        ]
        for copy in copies:
            copy.start()
        return copies

    def finish(copies):
        for copy in copies:
            copy.wait()

    def pack(x, value, carry):
        last, first = carry
        last = jnp.where(lane == x + 1, pltpu.roll(value[:, width - LANES:], x + 2, 1), last)
        first = jnp.where(lane == x, pltpu.roll(value[:, :LANES], x, 1), first)
        return last, first

    def store_columns(phase, carry):
        col_send[phase, 0] = carry[0]
        col_send[phase, 1] = carry[1]

    empty = (jnp.zeros((n_rhs, LANES), F32), jnp.zeros((n_rhs, LANES), F32))

    def neighbours(phase, buf, x):
        cur = buf[x + 1]
        prev_t = pltpu.roll(col_recv[phase, 0], 127 - x, 1)
        back_t = pltpu.roll(col_recv[phase, 1], 127 - x, 1)
        parts = [cur[:, k * LANES:(k + 1) * LANES] for k in range(tiles)]
        right = [prev_t] + [pltpu.roll(p, 1, 1) for p in parts]
        left = [pltpu.roll(p, LANES - 1, 1) for p in parts] + [back_t]
        low = [jnp.where(lane == 0, right[k], right[k + 1]) for k in range(tiles)]
        high = [jnp.where(lane == LANES - 1, left[k + 1], left[k]) for k in range(tiles)]
        low = jnp.concatenate(low, axis=1)
        high = jnp.concatenate(high, axis=1)
        total = cf[AX, pl.ds(x, 1), :] * buf[x + 2] + cf[AX_LOW, pl.ds(x, 1), :] * buf[x]
        return cur, total + cf[AY, pl.ds(x, 1), :] * high + cf[AY_LOW, pl.ds(x, 1), :] * low

    def row(plane, x):
        return cf[plane, pl.ds(x, 1), :]

    def hot_of(x):
        return jnp.where(label == row(LABEL, x), 1.0, 0.0).astype(BF16)

    wx, wy, agg = face_ref[0], face_ref[1], agg_ref[...].astype(F32)
    xs = lax.broadcasted_iota(jnp.int32, (rows, width), 0)
    ys = lax.broadcasted_iota(jnp.int32, (rows, width), 1)
    wx_low = jnp.where(xs == 0, 0.0, pltpu.roll(wx, 1, 0))
    wy_low = jnp.where(ys == 0, 0.0, pltpu.roll(wy, 1, 1))
    own_diag = diag_ref[...] + wx + wy + wx_low + wy_low
    cf[LABEL] = agg
    cf[LABEL_X] = pltpu.roll(agg, rows - 1, 0)
    cf[LABEL_Y] = pltpu.roll(agg, width - 1, 1)
    cf[WX] = jnp.where(xs == rows - 1, 0.0, wx)
    cf[WY] = jnp.where(ys == width - 1, 0.0, wy)
    cf[HALF] = 0.5 * own_diag
    acc[...] = jnp.zeros_like(acc)

    pl.semaphore_wait(barrier, n_member + 1)
    edges = [
        remote(s, d, edge_ssem.at[i], edge_rsem.at[i], t)
        for i, (s, d, t) in enumerate((
            (face_ref.at[0, pl.ds(rows - 8, 8), :], low_row_ref, (g_up, mi)),
            (face_ref.at[1, :, pl.ds(width - LANES, LANES)], below_w_ref, (gi, m_up)),
            (agg_ref.at[:, pl.ds(width - LANES, LANES)], below_a_ref, (gi, m_up)),
            (agg_ref.at[:, pl.ds(0, LANES)], above_a_ref, (gi, m_down)),
        ))
    ]
    for copy in edges:
        copy.start()

    def pairs(block, carry):
        total = jnp.zeros(acc.shape, F32)
        for i in range(D_BLOCK):
            x = block * D_BLOCK + i
            own = label == row(LABEL, x)
            hot = jnp.where(own, 1.0, 0.0).astype(BF16)
            value = jnp.where(own, row(HALF, x), 0.0)
            value = value - jnp.where(label == row(LABEL_X, x), row(WX, x), 0.0)
            value = value - jnp.where(label == row(LABEL_Y, x), row(WY, x), 0.0)
            high, low = split(value)
            both = jnp.concatenate([high, low], axis=0)
            total = total + lax.dot_general(hot, both, NT, preferred_element_type=F32)
        acc[...] += total
        return carry

    blocks = rows // D_BLOCK
    early = blocks * 5 // 8
    lax.fori_loop(0, early, pairs, 0)
    finish(edges)

    low_row = jnp.where(gi > 0, low_row_ref[7:8, :], 0.0)
    below = jnp.where(mi > 0, below_w_ref[:, LANES - 1:], 0.0)
    wx_low = wx_low + jnp.where(xs == 0, low_row, 0.0)
    wy_low = wy_low + jnp.where(ys == 0, below, 0.0)
    diagf = diag_ref[...] + wx + wy + wx_low + wy_low
    q = OMEGA / diagf
    last_x = (xs == rows - 1) & (gi == n_group - 1)
    last_y = (ys == width - 1) & (mi == n_member - 1)
    cf[AX] = jnp.where(last_x, 0.0, q * wx)
    cf[AX_LOW] = q * wx_low
    cf[AY] = jnp.where(last_y, 0.0, q * wy)
    cf[AY_LOW] = q * wy_low
    cf[Q] = q
    cf[Q_INV] = diagf * (1.0 / OMEGA)

    def scale(x, carry):
        fetch(x).wait()
        value = rhs[x] * row(Q, x)
        b[x + 1] = value
        return pack(x, value, carry)

    store_columns(0, lax.fori_loop(0, rows, scale, empty, unroll=2))
    first = exchange(0, b)
    lax.fori_loop(early, blocks, pairs, 0)

    def dot_high(left, right):
        return jnp.dot(
            left, right, precision=lax.Precision.HIGHEST, preferred_element_type=F32
        )

    lab = lax.broadcasted_iota(jnp.int32, (rows, LANES), 1)

    def hot_column(column):
        return jnp.where(column == lab, 1.0, 0.0)

    first_hot = hot_column(agg_ref[:, 0:1])
    last_hot = hot_column(agg_ref[:, width - 1:])
    below_hot = hot_column(below_a_ref[:, LANES - 1:])
    above_hot = hot_column(above_a_ref[:, 0:1])
    above = jnp.where(mi < n_member - 1, face_ref[1, :, width - 1:], 0.0)
    half = acc[:, :AGG] + acc[:, AGG:]
    half = half + dot_high(first_hot.T, first_hot * (0.5 * below))
    own = label == row(LABEL, 0)
    low_sum = jnp.sum(jnp.where(own, low_row, 0.0), axis=1, keepdims=True)
    eye = lax.broadcasted_iota(jnp.int32, (AGG, AGG), 0)
    eye = eye == lax.broadcasted_iota(jnp.int32, (AGG, AGG), 1)
    half = half + jnp.where(eye, 0.5 * low_sum, 0.0)
    w = jnp.concatenate(
        [
            half + half.T,
            -dot_high(below_hot.T, first_hot * below),
            -dot_high(above_hot.T, last_hot * above),
        ],
        axis=0,
    )
    lm = jnp.sum(jnp.abs(w), axis=0, keepdims=True)
    lm_send[...] = jnp.broadcast_to(lm, lm_send.shape)
    lm_copies = []
    for off in range(1, n_member):
        peer = lax.rem(mi + off, n_member)
        copy = remote(
            lm_send, lm_recv.at[off - 1], lm_ssem.at[off - 1], lm_rsem.at[off - 1], (gi, peer)
        )
        copy.start()
        lm_copies.append(copy)
    w_high, w_low = split(w)
    finish(first)

    def pre(x, carry):
        cur, total = neighbours(0, b, x)
        value = (2.0 - OMEGA) * cur + total
        f[x + 1] = value
        return pack(x, value, carry)

    store_columns(1, lax.fori_loop(0, rows, pre, empty, unroll=2))
    finish(exchange(1, f))

    def restrict(x, carry):
        cur, total = neighbours(1, f, x)
        resid = (b[x + 1] - OMEGA * cur + total) * row(Q_INV, x)
        high, low = split(resid)
        both = jnp.concatenate([high, low], axis=0)
        return carry + lax.dot_general(both, hot_of(x), NT, preferred_element_type=F32)

    sums = lax.fori_loop(0, rows, restrict, jnp.zeros((2 * n_rhs, AGG), F32), unroll=4)
    resid = sums[:n_rhs] + sums[n_rhs:]

    for copy in lm_copies:
        copy.wait()
    lm8 = lm_send[...]
    for off in range(1, n_member):
        lm8 = jnp.maximum(lm8, lm_recv[off - 1])
    lmax = jnp.max(lm8[0:1], axis=1, keepdims=True)
    lmin = lmax / RATIO
    theta = (lmax + lmin) / 2.0
    delta = (lmax - lmin) / 2.0
    sigma = theta / delta
    rho = 1.0 / sigma
    direc = resid / theta
    sol = jnp.zeros_like(resid)
    for step in range(CHEB):
        if step + 1 < CHEB:
            dir_send[step] = direc
            copies = [
                remote(
                    dir_send.at[step], dir_recv.at[step, i],
                    dir_ssem.at[step, i], dir_rsem.at[step, i], (gi, peer),
                )
                for i, peer in enumerate((m_up, m_down))
            ]
            for copy in copies:
                copy.start()
            sol = sol + direc
            rho_new = 1.0 / (2.0 * sigma - rho)
            finish(copies)
            vec = jnp.concatenate([direc, dir_recv[step, 0], dir_recv[step, 1]], axis=1)
            v_high, v_low = split(vec)
            both = jnp.concatenate([v_high, v_low], axis=0)
            prod = jnp.dot(both, w_high, preferred_element_type=F32)
            prod = prod[:n_rhs] + prod[n_rhs:]
            prod = prod + jnp.dot(v_high, w_low, preferred_element_type=F32)
            resid = resid - prod
            direc = rho_new * rho * direc + (2.0 * rho_new / delta) * resid
            rho = rho_new
        else:
            sol = sol + direc

    e_high, e_low = split(sol)
    e_both = jnp.concatenate([e_high, e_low], axis=0)

    def prolong(x, carry):
        spread = jnp.dot(e_both, hot_of(x), preferred_element_type=F32)
        value = f[x + 1] + spread[:n_rhs] + spread[n_rhs:]
        g[x + 1] = value
        return pack(x, value, carry)

    store_columns(2, lax.fori_loop(0, rows, prolong, empty, unroll=4))
    finish(exchange(2, g))

    def post(x, carry):
        cur, total = neighbours(2, g, x)
        value = b[x + 1] + (1.0 - OMEGA) * cur + total
        h[x + 1] = value
        return pack(x, value, carry)

    store_columns(3, lax.fori_loop(0, rows, post, empty, unroll=2))
    finish(exchange(3, h))

    def final(x, carry):
        cur, total = neighbours(3, h, x)
        out_ref[x] = b[x + 1] + (1.0 - OMEGA) * cur + total
        return carry

    lax.fori_loop(0, rows, final, 0, unroll=2)


def local(right_side, diagonal, face_weight, aggregation):
    n_group, n_member = lax.axis_size("group"), lax.axis_size("member")
    n_rhs, rows, width = right_side.shape
    padded = pltpu.VMEM((rows + 2, n_rhs, width), F32)
    dma = pltpu.SemaphoreType.DMA
    vmem = pl.BlockSpec(memory_space=pltpu.VMEM)
    out = pl.pallas_call(
        functools.partial(cycle_kernel, n_group, n_member),
        out_shape=jax.ShapeDtypeStruct((rows, n_rhs, width), F32),
        in_specs=[pl.BlockSpec(memory_space=pl.ANY), vmem, vmem, vmem],
        out_specs=vmem,
        scratch_shapes=[
            pltpu.VMEM((rows, n_rhs, width), F32),
            pltpu.VMEM((12, rows, width), F32),
            pltpu.VMEM((AGG, 2 * AGG), F32),
            pltpu.VMEM((8, width), F32),
            pltpu.VMEM((rows, LANES), F32),
            pltpu.VMEM((rows, LANES), jnp.int32),
            pltpu.VMEM((rows, LANES), jnp.int32),
            padded, padded, padded, padded,
            pltpu.VMEM((4, 2, n_rhs, LANES), F32),
            pltpu.VMEM((4, 2, n_rhs, LANES), F32),
            pltpu.VMEM((CHEB - 1, n_rhs, AGG), F32),
            pltpu.VMEM((CHEB - 1, 2, n_rhs, AGG), F32),
            pltpu.VMEM((8, AGG), F32),
            pltpu.VMEM((n_member - 1, 8, AGG), F32),
            dma((rows,)), dma((4,)), dma((4,)),
            dma((4, 4)), dma((4, 4)),
            dma((CHEB - 1, 2)), dma((CHEB - 1, 2)),
            dma((n_member - 1,)), dma((n_member - 1,)),
        ],
        compiler_params=pltpu.CompilerParams(
            collective_id=0, has_side_effects=True, vmem_limit_bytes=48 * 1024 * 1024
        ),
    )(right_side, diagonal, face_weight, aggregation)
    return out.transpose(1, 0, 2)


def solution(mesh):
    placed = (
        P(None, "group", "member"),
        P("group", "member"),
        P(None, "group", "member"),
        P("group", "member"),
    )
    return jax.shard_map(
        local, mesh=mesh, in_specs=placed, out_specs=P(None, "group", "member"), check_vma=False
    )
```

time: 119 us -> 94.5 us (0.79)
  local copies, waits for them, and re-layouts: 21.2 us -> 7.2 us
  starting transfers between devices: 8.52 us -> 0 us
  other arithmetic: 2.6 us -> 0 us
  Pallas kernels: 85.5 us -> 87.2 us
    pallas_call x1, Pallas kernels: 74.5 us -> 87.2 us  [local(): pl.pallas_call(functools.partial(cycle_kernel, n_group, n_member), out_sh...]
    pallas_call x1 -> x0, Pallas kernels: 11 us -> none  [local(): pl.pallas_call(functools.partial(coarse_kernel, block), grid=(rows // blo...]
    ppermute x3 -> x0, starting transfers between devices: 8.52 us -> none  [passed_along(): lax.ppermute(value, axis, [(source, source + steps) for source in range(i...]
    another operation x14 -> x0, local copies, waits for them, and re-layouts: 5.56 us -> none  [the longest x4 2.92 us: local(): jnp.stack([agg, agg_x, agg_y, 0.5 * diagf, jnp.where(xs == rows - 1, 0.0,...]
    unnamed x7 -> x6, local copies, waits for them, and re-layouts: 7.61 us -> 2.76 us
    slice x7 -> x0, local copies, waits for them, and re-layouts: 2.84 us -> none  [the longest x1 0.93 us: local(): wy = face_weight[1]]
  transfers between devices with their start and end apart: 3 -> 0, of which waited for: 0 -> 0; matrix products, arithmetic and copies ran while one was open for 10% -> 0% of each run, Pallas kernels for 0% -> 0%
where the time goes in v1:
time: 94.5 us; the launch traced here: 94.4 us
  Pallas kernels  87.2 us (92%)
  local copies, waits for them, and re-layouts  7.2 us (8%)
    pallas_call x1, Pallas kernels, local(): pl.pallas_call(functools.partial(cycle_kernel, n_group, n_member), out_sh...  87.2 us
    transpose x1, local copies, waits for them, and re-layouts, local(): return out.transpose(1, 0, 2)  4.44 us
    unnamed x6, local copies, waits for them, and re-layouts  2.76 us

profile of v1, /device:TPU:0, one launch (start us, length us, event | category | flops | bytes accessed | tf_op | source)
XLA Modules:
  0.0 94.4 jit_solution(3718469255283791152)
XLA Ops:
  0.0 0.0 copy-start
  0.0 0.9 %copy-done = f32[2,64,512]{2,1,0:T(8,128)S(1)} copy-done((f32[2,64,512]{2,1,0:T(8,128)S(1)}, f32[2,64,512]{2,1,0:T(8,128)}, u32[]{:S(2)}) %copy-start) | copy-done | bytes 262168
  1.0 0.0 copy-start.1
  1.0 0.9 copy-done.1
  1.9 0.0 copy-start.2
  1.9 0.9 copy-done.2
  2.8 87.2 %shard_map.46 = f32[64,32,512]{2,1,0:T(8,128)S(1)} custom-call(f32[32,64,512]{2,1,0:T(8,128)} %rhs_hbm.1, f32[64,512]{1,0:T(8,128)S(1)} %copy-done.1, f32[2,64,512]{2,1,0:T(8,128)S(1)} %copy-done, s32[64,512]{1,0:T(8,128)S(1)} %copy-done.2), custom_call_target="tpu_custom_call" | custom-call | tf_op jit(solution)/shard_map/pallas_call | solution.py:329
  89.9 4.4 %copy.5 = f32[32,64,512]{2,1,0:T(8,128)} copy(f32[32,64,512]{2,0,1:T(8,128)S(1)} %bitcast.1) | data formatting | bytes 8388608 | tf_op jit(solution)/shard_map/transpose | solution.py:358
Async XLA Ops:
  0.0 0.9 %copy-start = (f32[2,64,512]{2,1,0:T(8,128)S(1)}, f32[2,64,512]{2,1,0:T(8,128)}, u32[]{:S(2)}) copy-start(f32[2,64,512]{2,1,0:T(8,128)} %face_ref.1) | copy-start | bytes 786436
  1.0 0.9 copy-start.1
  1.9 0.9 copy-start.2

commit v2 on v1

--- a/solution.py
+++ b/solution.py
@@ -81,13 +81,16 @@
             copy.start()
         return copies
 
+    started = []
+
     def finish(copies):
         for copy in copies:
-            copy.wait()
+            copy.wait_recv()
+        started.extend(copies)
 
     def pack(x, value, carry):
         last, first = carry
-        last = jnp.where(lane == x + 1, pltpu.roll(value[:, width - LANES:], x + 2, 1), last)
+        last = jnp.where(lane == x + 1, pltpu.roll(value[:, value.shape[1] - LANES:], x + 2, 1), last)
         first = jnp.where(lane == x, pltpu.roll(value[:, :LANES], x, 1), first)
         return last, first
 
@@ -97,19 +100,45 @@
 
     empty = (jnp.zeros((n_rhs, LANES), F32), jnp.zeros((n_rhs, LANES), F32))
 
-    def neighbours(phase, buf, x):
+    def neighbours(buf, x):
         cur = buf[x + 1]
-        prev_t = pltpu.roll(col_recv[phase, 0], 127 - x, 1)
-        back_t = pltpu.roll(col_recv[phase, 1], 127 - x, 1)
         parts = [cur[:, k * LANES:(k + 1) * LANES] for k in range(tiles)]
-        right = [prev_t] + [pltpu.roll(p, 1, 1) for p in parts]
-        left = [pltpu.roll(p, LANES - 1, 1) for p in parts] + [back_t]
+        zero = jnp.zeros((n_rhs, LANES), F32)
+        right = [zero] + [pltpu.roll(p, 1, 1) for p in parts]
+        left = [pltpu.roll(p, LANES - 1, 1) for p in parts] + [zero]
         low = [jnp.where(lane == 0, right[k], right[k + 1]) for k in range(tiles)]
         high = [jnp.where(lane == LANES - 1, left[k + 1], left[k]) for k in range(tiles)]
         low = jnp.concatenate(low, axis=1)
         high = jnp.concatenate(high, axis=1)
         total = cf[AX, pl.ds(x, 1), :] * buf[x + 2] + cf[AX_LOW, pl.ds(x, 1), :] * buf[x]
         return cur, total + cf[AY, pl.ds(x, 1), :] * high + cf[AY_LOW, pl.ds(x, 1), :] * low
+
+    def patch(phase, x):
+        before = pltpu.roll(col_recv[phase, 0], 127 - x, 1)
+        after = pltpu.roll(col_recv[phase, 1], 127 - x, 1)
+        low = jnp.where(lane == 0, before, 0.0) * cf[AY_LOW, pl.ds(x, 1), :][:, :LANES]
+        high = jnp.where(lane == LANES - 1, after, 0.0) * cf[AY, pl.ds(x, 1), :][:, width - LANES:]
+        return low, high
+
+    def sweep(phase, copies, body, dest, shift, unroll):
+        def inner(x, carry):
+            dest[x + shift] = body(x)
+            return carry
+
+        lax.fori_loop(1, rows - 1, inner, 0, unroll=unroll)
+        finish(copies)
+        inner(0, 0)
+        inner(rows - 1, 0)
+
+        def outer(x, carry):
+            low, high = patch(phase, x)
+            first = dest[x + shift, :, :LANES] + low
+            last = dest[x + shift, :, width - LANES:] + high
+            dest[x + shift, :, :LANES] = first
+            dest[x + shift, :, width - LANES:] = last
+            return pack(x, jnp.concatenate([first, last], axis=1), carry)
+
+        return lax.fori_loop(0, rows, outer, empty, unroll=4)
 
     def row(plane, x):
         return cf[plane, pl.ds(x, 1), :]
@@ -230,29 +259,33 @@
         copy.start()
         lm_copies.append(copy)
     w_high, w_low = split(w)
-    finish(first)
-
-    def pre(x, carry):
-        cur, total = neighbours(0, b, x)
-        value = (2.0 - OMEGA) * cur + total
-        f[x + 1] = value
-        return pack(x, value, carry)
-
-    store_columns(1, lax.fori_loop(0, rows, pre, empty, unroll=2))
-    finish(exchange(1, f))
+
+    def pre(x):
+        cur, total = neighbours(b, x)
+        return (2.0 - OMEGA) * cur + total
+
+    store_columns(1, sweep(0, first, pre, f, 1, 2))
+    second = exchange(1, f)
 
     def restrict(x, carry):
-        cur, total = neighbours(1, f, x)
+        cur, total = neighbours(f, x)
         resid = (b[x + 1] - OMEGA * cur + total) * row(Q_INV, x)
         high, low = split(resid)
         both = jnp.concatenate([high, low], axis=0)
         return carry + lax.dot_general(both, hot_of(x), NT, preferred_element_type=F32)
 
-    sums = lax.fori_loop(0, rows, restrict, jnp.zeros((2 * n_rhs, AGG), F32), unroll=4)
+    sums = lax.fori_loop(
+        1, rows - 1, restrict, jnp.zeros((2 * n_rhs, AGG), F32), unroll=2
+    )
+    finish(second)
+    sums = restrict(rows - 1, restrict(0, sums))
     resid = sums[:n_rhs] + sums[n_rhs:]
-
-    for copy in lm_copies:
-        copy.wait()
+    resid = resid + dot_high(
+        pltpu.roll(col_recv[1, 0], LANES - 1, 1)[:, :rows], first_hot * below
+    )
+    resid = resid + dot_high(col_recv[1, 1][:, :rows], last_hot * above)
+
+    finish(lm_copies)
     lm8 = lm_send[...]
     for off in range(1, n_member):
         lm8 = jnp.maximum(lm8, lm_recv[off - 1])
@@ -301,23 +334,22 @@
         return pack(x, value, carry)
 
     store_columns(2, lax.fori_loop(0, rows, prolong, empty, unroll=4))
-    finish(exchange(2, g))
-
-    def post(x, carry):
-        cur, total = neighbours(2, g, x)
-        value = b[x + 1] + (1.0 - OMEGA) * cur + total
-        h[x + 1] = value
-        return pack(x, value, carry)
-
-    store_columns(3, lax.fori_loop(0, rows, post, empty, unroll=2))
-    finish(exchange(3, h))
-
-    def final(x, carry):
-        cur, total = neighbours(3, h, x)
-        out_ref[x] = b[x + 1] + (1.0 - OMEGA) * cur + total
-        return carry
-
-    lax.fori_loop(0, rows, final, 0, unroll=2)
+    third = exchange(2, g)
+
+    def post(x):
+        cur, total = neighbours(g, x)
+        return b[x + 1] + (1.0 - OMEGA) * cur + total
+
+    store_columns(3, sweep(2, third, post, h, 1, 2))
+    fourth = exchange(3, h)
+
+    def final(x):
+        cur, total = neighbours(h, x)
+        return b[x + 1] + (1.0 - OMEGA) * cur + total
+
+    sweep(3, fourth, final, out_ref, 0, 2)
+    for copy in started:
+        copy.wait_send()
 
 
 def local(right_side, diagonal, face_weight, aggregation):

time: 94.5 us -> 86.4 us (0.914)
  Pallas kernels: 87.2 us -> 79 us
    pallas_call x1, Pallas kernels: 87.2 us -> 79 us  [local(): pl.pallas_call(functools.partial(cycle_kernel, n_group, n_member), out_sh...]
where the time goes in v2:
time: 86.4 us; the launch traced here: 86.2 us
  Pallas kernels  79 us (91%)
  local copies, waits for them, and re-layouts  7.2 us (8%)
    pallas_call x1, Pallas kernels, local(): pl.pallas_call(functools.partial(cycle_kernel, n_group, n_member), out_sh...  79 us
    transpose x1, local copies, waits for them, and re-layouts, local(): return out.transpose(1, 0, 2)  4.44 us
    unnamed x6, local copies, waits for them, and re-layouts  2.76 us

profile of v2, /device:TPU:0, one launch (start us, length us, event | category | flops | bytes accessed | tf_op | source)
XLA Modules:
  0.0 86.2 jit_solution(2738383423072697613)
XLA Ops:
  0.0 0.0 copy-start
  0.0 0.9 %copy-done = f32[2,64,512]{2,1,0:T(8,128)S(1)} copy-done((f32[2,64,512]{2,1,0:T(8,128)S(1)}, f32[2,64,512]{2,1,0:T(8,128)}, u32[]{:S(2)}) %copy-start) | copy-done | bytes 262168
  1.0 0.0 copy-start.1
  1.0 0.9 %copy-done.1 = f32[64,512]{1,0:T(8,128)S(1)} copy-done((f32[64,512]{1,0:T(8,128)S(1)}, f32[64,512]{1,0:T(8,128)}, u32[]{:S(2)}) %copy-start.1) | copy-done | bytes 131096
  1.9 0.0 copy-start.2
  1.9 0.9 %copy-done.2 = s32[64,512]{1,0:T(8,128)S(1)} copy-done((s32[64,512]{1,0:T(8,128)S(1)}, s32[64,512]{1,0:T(8,128)}, u32[]{:S(2)}) %copy-start.2) | copy-done | bytes 131096
  2.8 79.0 %shard_map.46 = f32[64,32,512]{2,1,0:T(8,128)S(1)} custom-call(f32[32,64,512]{2,1,0:T(8,128)} %rhs_hbm.1, f32[64,512]{1,0:T(8,128)S(1)} %copy-done.1, f32[2,64,512]{2,1,0:T(8,128)S(1)} %copy-done, s32[64,512]{1,0:T(8,128)S(1)} %copy-done.2), custom_call_target="tpu_custom_call" | custom-call | tf_op jit(solution)/shard_map/pallas_call | solution.py:361
  81.8 4.4 %copy.5 = f32[32,64,512]{2,1,0:T(8,128)} copy(f32[32,64,512]{2,0,1:T(8,128)S(1)} %bitcast.1) | data formatting | bytes 8388608 | tf_op jit(solution)/shard_map/transpose | solution.py:390
Async XLA Ops:
  0.0 0.9 %copy-start = (f32[2,64,512]{2,1,0:T(8,128)S(1)}, f32[2,64,512]{2,1,0:T(8,128)}, u32[]{:S(2)}) copy-start(f32[2,64,512]{2,1,0:T(8,128)} %face_ref.1) | copy-start | bytes 786436
  1.0 0.9 %copy-start.1 = (f32[64,512]{1,0:T(8,128)S(1)}, f32[64,512]{1,0:T(8,128)}, u32[]{:S(2)}) copy-start(f32[64,512]{1,0:T(8,128)} %diag_ref.1) | copy-start | bytes 393220
  1.9 0.9 %copy-start.2 = (s32[64,512]{1,0:T(8,128)S(1)}, s32[64,512]{1,0:T(8,128)}, u32[]{:S(2)}) copy-start(s32[64,512]{1,0:T(8,128)} %agg_ref.1) | copy-start | bytes 393220

commit v3 on v2

--- a/solution.py
+++ b/solution.py
@@ -26,13 +26,16 @@
 
 AX, AX_LOW, AY, AY_LOW, Q, Q_INV, LABEL, LABEL_X, LABEL_Y, WX, WY, HALF = range(12)
 D_BLOCK = 4
+NEAR = (-2, -1, 1, 2)
+FAR = (-3, -2, -1, 1, 2, 3)
 
 
 def cycle_kernel(
     n_group, n_member, rhs_hbm, diag_ref, face_ref, agg_ref, out_ref,
     rhs, cf, acc, low_row_ref, below_w_ref, below_a_ref, above_a_ref,
     b, f, g, h, col_send, col_recv, dir_send, dir_recv, lm_send, lm_recv,
-    rhs_sem, edge_ssem, edge_rsem, halo_ssem, halo_rsem, dir_ssem, dir_rsem, lm_ssem, lm_rsem,
+    w_send, w_recv, state_send, state_recv,
+    rhs_sem, w_ssem, w_rsem, state_ssem, state_rsem, edge_ssem, edge_rsem, halo_ssem, halo_rsem, dir_ssem, dir_rsem, lm_ssem, lm_rsem,
 ):
     rows, n_rhs, width = rhs.shape
     tiles = width // LANES
@@ -40,6 +43,9 @@
     mi = lax.axis_index("member")
     g_up, g_down = lax.rem(gi + 1, n_group), lax.rem(gi + n_group - 1, n_group)
     m_up, m_down = lax.rem(mi + 1, n_member), lax.rem(mi + n_member - 1, n_member)
+
+    def member_at(off):
+        return lax.rem(mi + off + n_member, n_member)
 
     def fetch(x):
         return pltpu.make_async_copy(rhs_hbm.at[:, x, :], rhs.at[x], rhs_sem.at[x])
@@ -258,7 +264,13 @@
         )
         copy.start()
         lm_copies.append(copy)
-    w_high, w_low = split(w)
+    w_send[...] = w
+    w_copies = {}
+    for i, off in enumerate(NEAR):
+        w_copies[-off] = (i, remote(
+            w_send, w_recv.at[i], w_ssem.at[i], w_rsem.at[i], (gi, member_at(off))
+        ))
+        w_copies[-off][1].start()
 
     def pre(x):
         cur, total = neighbours(b, x)
@@ -295,34 +307,56 @@
     delta = (lmax - lmin) / 2.0
     sigma = theta / delta
     rho = 1.0 / sigma
-    direc = resid / theta
+    finish([copy for _, copy in w_copies.values()])
+    blocks_w = {0: split(w_send[...])}
+    for off, (i, _) in w_copies.items():
+        blocks_w[off] = split(w_recv[i])
+
+    def product(at, dirs):
+        w_high, w_low = blocks_w[at]
+        vec = jnp.concatenate([dirs[at], dirs[at - 1], dirs[at + 1]], axis=1)
+        v_high, v_low = split(vec)
+        both = jnp.concatenate([v_high, v_low], axis=0)
+        prod = jnp.dot(both, w_high, preferred_element_type=F32)
+        prod = prod[:n_rhs] + prod[n_rhs:]
+        return prod + jnp.dot(v_high, w_low, preferred_element_type=F32)
+
+    def gather(send, recv, ssem, rsem, offsets):
+        copies = [
+            remote(send, recv.at[i], ssem.at[i], rsem.at[i], (gi, member_at(off)))
+            for i, off in enumerate(offsets)
+        ]
+        for copy in copies:
+            copy.start()
+        finish(copies)
+
+    dirs = {0: resid / theta}
+    dir_send[...] = dirs[0]
+    gather(dir_send, dir_recv, dir_ssem, dir_rsem, FAR)
+    res = {0: resid}
+    for i, off in enumerate(FAR):
+        dirs[-off] = dir_recv[i]
+        res[-off] = dirs[-off] * theta
+    reach = 3
     sol = jnp.zeros_like(resid)
     for step in range(CHEB):
+        sol = sol + dirs[0]
         if step + 1 < CHEB:
-            dir_send[step] = direc
-            copies = [
-                remote(
-                    dir_send.at[step], dir_recv.at[step, i],
-                    dir_ssem.at[step, i], dir_rsem.at[step, i], (gi, peer),
-                )
-                for i, peer in enumerate((m_up, m_down))
-            ]
-            for copy in copies:
-                copy.start()
-            sol = sol + direc
+            if reach == 0:
+                state_send[0] = dirs[0]
+                state_send[1] = res[0]
+                gather(state_send, state_recv, state_ssem, state_rsem, NEAR)
+                for i, off in enumerate(NEAR):
+                    dirs[-off] = state_recv[i, 0]
+                    res[-off] = state_recv[i, 1]
+                reach = 2
+            reach -= 1
             rho_new = 1.0 / (2.0 * sigma - rho)
-            finish(copies)
-            vec = jnp.concatenate([direc, dir_recv[step, 0], dir_recv[step, 1]], axis=1)
-            v_high, v_low = split(vec)
-            both = jnp.concatenate([v_high, v_low], axis=0)
-            prod = jnp.dot(both, w_high, preferred_element_type=F32)
-            prod = prod[:n_rhs] + prod[n_rhs:]
-            prod = prod + jnp.dot(v_high, w_low, preferred_element_type=F32)
-            resid = resid - prod
-            direc = rho_new * rho * direc + (2.0 * rho_new / delta) * resid
+            own_scale, res_scale = rho_new * rho, 2.0 * rho_new / delta
+            inside = range(-reach, reach + 1)
+            res = {at: res[at] - product(at, dirs) for at in inside}
+            dirs = {at: own_scale * dirs[at] + res_scale * res[at] for at in inside}
             rho = rho_new
-        else:
-            sol = sol + direc
 
     e_high, e_low = split(sol)
     e_both = jnp.concatenate([e_high, e_low], axis=0)
@@ -374,13 +408,18 @@
             padded, padded, padded, padded,
             pltpu.VMEM((4, 2, n_rhs, LANES), F32),
             pltpu.VMEM((4, 2, n_rhs, LANES), F32),
-            pltpu.VMEM((CHEB - 1, n_rhs, AGG), F32),
-            pltpu.VMEM((CHEB - 1, 2, n_rhs, AGG), F32),
+            pltpu.VMEM((n_rhs, AGG), F32),
+            pltpu.VMEM((len(FAR), n_rhs, AGG), F32),
             pltpu.VMEM((8, AGG), F32),
             pltpu.VMEM((n_member - 1, 8, AGG), F32),
-            dma((rows,)), dma((4,)), dma((4,)),
+            pltpu.VMEM((3 * AGG, AGG), F32),
+            pltpu.VMEM((len(NEAR), 3 * AGG, AGG), F32),
+            pltpu.VMEM((2, n_rhs, AGG), F32),
+            pltpu.VMEM((len(NEAR), 2, n_rhs, AGG), F32),
+            dma((rows,)), dma((len(NEAR),)), dma((len(NEAR),)),
+            dma((len(NEAR),)), dma((len(NEAR),)), dma((4,)), dma((4,)),
             dma((4, 4)), dma((4, 4)),
-            dma((CHEB - 1, 2)), dma((CHEB - 1, 2)),
+            dma((len(FAR),)), dma((len(FAR),)),
             dma((n_member - 1,)), dma((n_member - 1,)),
         ],
         compiler_params=pltpu.CompilerParams(

time: 86.4 us -> 76.2 us (0.88)
  Pallas kernels: 79 us -> 68.8 us
    pallas_call x1, Pallas kernels: 79 us -> 68.8 us  [local(): pl.pallas_call(functools.partial(cycle_kernel, n_group, n_member), out_sh...]
where the time goes in v3:
time: 76.2 us; the launch traced here: 76 us
  Pallas kernels  68.8 us (90%)
  local copies, waits for them, and re-layouts  7.2 us (9%)
    pallas_call x1, Pallas kernels, local(): pl.pallas_call(functools.partial(cycle_kernel, n_group, n_member), out_sh...  68.8 us
    transpose x1, local copies, waits for them, and re-layouts, local(): return out.transpose(1, 0, 2)  4.44 us
    unnamed x6, local copies, waits for them, and re-layouts  2.76 us

profile of v3, /device:TPU:0, one launch (start us, length us, event | category | flops | bytes accessed | tf_op | source)
XLA Modules:
  0.0 76.0 jit_solution(1114551098070091597)
XLA Ops:
  0.0 0.0 copy-start
  0.0 0.9 %copy-done = f32[2,64,512]{2,1,0:T(8,128)S(1)} copy-done((f32[2,64,512]{2,1,0:T(8,128)S(1)}, f32[2,64,512]{2,1,0:T(8,128)}, u32[]{:S(2)}) %copy-start) | copy-done | bytes 262168
  1.0 0.0 copy-start.1
  1.0 0.9 %copy-done.1 = f32[64,512]{1,0:T(8,128)S(1)} copy-done((f32[64,512]{1,0:T(8,128)S(1)}, f32[64,512]{1,0:T(8,128)}, u32[]{:S(2)}) %copy-start.1) | copy-done | bytes 131096
  1.9 0.0 copy-start.2
  1.9 0.9 %copy-done.2 = s32[64,512]{1,0:T(8,128)S(1)} copy-done((s32[64,512]{1,0:T(8,128)S(1)}, s32[64,512]{1,0:T(8,128)}, u32[]{:S(2)}) %copy-start.2) | copy-done | bytes 131096
  2.8 68.8 %shard_map.46 = f32[64,32,512]{2,1,0:T(8,128)S(1)} custom-call(f32[32,64,512]{2,1,0:T(8,128)} %rhs_hbm.1, f32[64,512]{1,0:T(8,128)S(1)} %copy-done.1, f32[2,64,512]{2,1,0:T(8,128)S(1)} %copy-done, s32[64,512]{1,0:T(8,128)S(1)} %copy-done.2), custom_call_target="tpu_custom_call" | custom-call | tf_op jit(solution)/shard_map/pallas_call | solution.py:395
  71.6 4.4 %copy.5 = f32[32,64,512]{2,1,0:T(8,128)} copy(f32[32,64,512]{2,0,1:T(8,128)S(1)} %bitcast.1) | data formatting | bytes 8388608 | tf_op jit(solution)/shard_map/transpose | solution.py:429
Async XLA Ops:
  0.0 0.9 %copy-start = (f32[2,64,512]{2,1,0:T(8,128)S(1)}, f32[2,64,512]{2,1,0:T(8,128)}, u32[]{:S(2)}) copy-start(f32[2,64,512]{2,1,0:T(8,128)} %face_ref.1) | copy-start | bytes 786436
  1.0 0.9 %copy-start.1 = (f32[64,512]{1,0:T(8,128)S(1)}, f32[64,512]{1,0:T(8,128)}, u32[]{:S(2)}) copy-start(f32[64,512]{1,0:T(8,128)} %diag_ref.1) | copy-start | bytes 393220
  1.9 0.9 %copy-start.2 = (s32[64,512]{1,0:T(8,128)S(1)}, s32[64,512]{1,0:T(8,128)}, u32[]{:S(2)}) copy-start(s32[64,512]{1,0:T(8,128)} %agg_ref.1) | copy-start | bytes 393220

commit v4 on v3

--- a/solution.py
+++ b/solution.py
@@ -31,8 +31,8 @@
 
 
 def cycle_kernel(
-    n_group, n_member, rhs_hbm, diag_ref, face_ref, agg_ref, out_ref,
-    rhs, cf, acc, low_row_ref, below_w_ref, below_a_ref, above_a_ref,
+    n_group, n_member, rhs_hbm, diag_hbm, face_hbm, agg_hbm, out_hbm,
+    diag_ref, face_ref, agg_ref, in_sem, out_sem, rhs, cf, acc, low_row_ref, below_w_ref, below_a_ref, above_a_ref,
     b, f, g, h, col_send, col_recv, dir_send, dir_recv, lm_send, lm_recv,
     w_send, w_recv, state_send, state_recv,
     rhs_sem, w_ssem, w_rsem, state_ssem, state_rsem, edge_ssem, edge_rsem, halo_ssem, halo_rsem, dir_ssem, dir_rsem, lm_ssem, lm_rsem,
@@ -54,6 +54,14 @@
         fetch(x).start()
         return carry
 
+    inputs = [
+        pltpu.make_async_copy(s, d, in_sem.at[i])
+        for i, (s, d) in enumerate(
+            ((agg_hbm, agg_ref), (face_hbm, face_ref), (diag_hbm, diag_ref))
+        )
+    ]
+    for copy in inputs:
+        copy.start()
     lax.fori_loop(0, rows, start_fetch, 0)
 
     barrier = pltpu.get_barrier_semaphore()
@@ -126,7 +134,7 @@
         high = jnp.where(lane == LANES - 1, after, 0.0) * cf[AY, pl.ds(x, 1), :][:, width - LANES:]
         return low, high
 
-    def sweep(phase, copies, body, dest, shift, unroll):
+    def sweep(phase, copies, body, dest, shift, unroll, done=None):
         def inner(x, carry):
             dest[x + shift] = body(x)
             return carry
@@ -142,6 +150,9 @@
             last = dest[x + shift, :, width - LANES:] + high
             dest[x + shift, :, :LANES] = first
             dest[x + shift, :, width - LANES:] = last
+            if done is not None:
+                done(x)
+                return carry
             return pack(x, jnp.concatenate([first, last], axis=1), carry)
 
         return lax.fori_loop(0, rows, outer, empty, unroll=4)
@@ -151,6 +162,9 @@
 
     def hot_of(x):
         return jnp.where(label == row(LABEL, x), 1.0, 0.0).astype(BF16)
+
+    for copy in inputs:
+        copy.wait()
 
     wx, wy, agg = face_ref[0], face_ref[1], agg_ref[...].astype(F32)
     xs = lax.broadcasted_iota(jnp.int32, (rows, width), 0)
@@ -195,8 +209,7 @@
         return carry
 
     blocks = rows // D_BLOCK
-    early = blocks * 5 // 8
-    lax.fori_loop(0, early, pairs, 0)
+    lax.fori_loop(0, blocks, pairs, 0)
     finish(edges)
 
     low_row = jnp.where(gi > 0, low_row_ref[7:8, :], 0.0)
@@ -222,7 +235,6 @@
 
     store_columns(0, lax.fori_loop(0, rows, scale, empty, unroll=2))
     first = exchange(0, b)
-    lax.fori_loop(early, blocks, pairs, 0)
 
     def dot_high(left, right):
         return jnp.dot(
@@ -381,7 +393,16 @@
         cur, total = neighbours(h, x)
         return b[x + 1] + (1.0 - OMEGA) * cur + total
 
-    sweep(3, fourth, final, out_ref, 0, 2)
+    def result(x):
+        return pltpu.make_async_copy(rhs.at[x], out_hbm.at[x], out_sem.at[x])
+
+    sweep(3, fourth, final, rhs, 0, 2, lambda x: result(x).start())
+
+    def wait_result(x, carry):
+        result(x).wait()
+        return carry
+
+    lax.fori_loop(0, rows, wait_result, 0)
     for copy in started:
         copy.wait_send()
 
@@ -391,13 +412,17 @@
     n_rhs, rows, width = right_side.shape
     padded = pltpu.VMEM((rows + 2, n_rhs, width), F32)
     dma = pltpu.SemaphoreType.DMA
-    vmem = pl.BlockSpec(memory_space=pltpu.VMEM)
+    anywhere = pl.BlockSpec(memory_space=pl.ANY)
     out = pl.pallas_call(
         functools.partial(cycle_kernel, n_group, n_member),
         out_shape=jax.ShapeDtypeStruct((rows, n_rhs, width), F32),
-        in_specs=[pl.BlockSpec(memory_space=pl.ANY), vmem, vmem, vmem],
-        out_specs=vmem,
+        in_specs=[anywhere] * 4,
+        out_specs=anywhere,
         scratch_shapes=[
+            pltpu.VMEM((rows, width), F32),
+            pltpu.VMEM((2, rows, width), F32),
+            pltpu.VMEM((rows, width), jnp.int32),
+            dma((3,)), dma((rows,)),
             pltpu.VMEM((rows, n_rhs, width), F32),
             pltpu.VMEM((12, rows, width), F32),
             pltpu.VMEM((AGG, 2 * AGG), F32),
@@ -423,7 +448,7 @@
             dma((n_member - 1,)), dma((n_member - 1,)),
         ],
         compiler_params=pltpu.CompilerParams(
-            collective_id=0, has_side_effects=True, vmem_limit_bytes=48 * 1024 * 1024
+            collective_id=0, has_side_effects=True, vmem_limit_bytes=60 * 1024 * 1024
         ),
     )(right_side, diagonal, face_weight, aggregation)
     return out.transpose(1, 0, 2)

time: 76.2 us -> 77.1 us (1.012)
  Pallas kernels: 68.8 us -> 70.3 us
    unnamed x6 -> x0, local copies, waits for them, and re-layouts: 2.76 us -> none
    transpose x1, local copies, waits for them, and re-layouts: 4.44 us -> 6.63 us  [local(): return out.transpose(1, 0, 2)]
    pallas_call x1, Pallas kernels: 68.8 us -> 70.3 us  [local(): pl.pallas_call(functools.partial(cycle_kernel, n_group, n_member), out_sh...]
where the time goes in v4:
time: 77.1 us; the launch traced here: 76.9 us
  Pallas kernels  70.3 us (91%)
  local copies, waits for them, and re-layouts  6.63 us (9%)
    pallas_call x1, Pallas kernels, local(): pl.pallas_call(functools.partial(cycle_kernel, n_group, n_member), out_sh...  70.3 us
    transpose x1, local copies, waits for them, and re-layouts, local(): return out.transpose(1, 0, 2)  6.63 us

profile of v4, /device:TPU:0, one launch (start us, length us, event | category | flops | bytes accessed | tf_op | source)
XLA Modules:
  0.0 76.9 jit_solution(16032643311053923421)
XLA Ops:
  0.0 70.3 %shard_map.46 = f32[64,32,512]{2,1,0:T(8,128)} custom-call(f32[32,64,512]{2,1,0:T(8,128)} %rhs_hbm.1, f32[64,512]{1,0:T(8,128)} %diag_hbm.1, f32[2,64,512]{2,1,0:T(8,128)} %face_hbm.1, s32[64,512]{1,0:T(8,128)} %agg_hbm.1), custom_call_target="tpu_custom_call" | custom-call | tf_op jit(solution)/shard_map/pallas_call | solution.py:416
  70.3 6.6 %copy.5 = f32[32,64,512]{2,1,0:T(8,128)} copy(f32[32,64,512]{2,0,1:T(8,128)} %bitcast.1) | data formatting | bytes 8388608 | tf_op jit(solution)/shard_map/transpose | solution.py:454

commit v5 on v3

--- a/solution.py
+++ b/solution.py
@@ -195,7 +195,7 @@
         return carry
 
     blocks = rows // D_BLOCK
-    early = blocks * 5 // 8
+    early = blocks
     lax.fori_loop(0, early, pairs, 0)
     finish(edges)
 
@@ -287,7 +287,7 @@
         return carry + lax.dot_general(both, hot_of(x), NT, preferred_element_type=F32)
 
     sums = lax.fori_loop(
-        1, rows - 1, restrict, jnp.zeros((2 * n_rhs, AGG), F32), unroll=2
+        1, rows - 1, restrict, jnp.zeros((2 * n_rhs, AGG), F32), unroll=4
     )
     finish(second)
     sums = restrict(rows - 1, restrict(0, sums))

time: 76.2 us -> 76.3 us (level)
  no operation moved by 1% of the time
where the time goes in v5:
time: 76.3 us; the launch traced here: 76.1 us
  Pallas kernels  68.9 us (90%)
  local copies, waits for them, and re-layouts  7.2 us (9%)
    pallas_call x1, Pallas kernels, local(): pl.pallas_call(functools.partial(cycle_kernel, n_group, n_member), out_sh...  68.9 us
    transpose x1, local copies, waits for them, and re-layouts, local(): return out.transpose(1, 0, 2)  4.44 us
    unnamed x6, local copies, waits for them, and re-layouts  2.76 us

profile of v5, /device:TPU:0, one launch (start us, length us, event | category | flops | bytes accessed | tf_op | source)
XLA Modules:
  0.0 76.1 jit_solution(12219963898864320474)
XLA Ops:
  0.0 0.0 copy-start
  0.0 0.9 %copy-done = f32[2,64,512]{2,1,0:T(8,128)S(1)} copy-done((f32[2,64,512]{2,1,0:T(8,128)S(1)}, f32[2,64,512]{2,1,0:T(8,128)}, u32[]{:S(2)}) %copy-start) | copy-done | bytes 262168
  1.0 0.0 copy-start.1
  1.0 0.9 %copy-done.1 = f32[64,512]{1,0:T(8,128)S(1)} copy-done((f32[64,512]{1,0:T(8,128)S(1)}, f32[64,512]{1,0:T(8,128)}, u32[]{:S(2)}) %copy-start.1) | copy-done | bytes 131096
  1.9 0.0 copy-start.2
  1.9 0.9 %copy-done.2 = s32[64,512]{1,0:T(8,128)S(1)} copy-done((s32[64,512]{1,0:T(8,128)S(1)}, s32[64,512]{1,0:T(8,128)}, u32[]{:S(2)}) %copy-start.2) | copy-done | bytes 131096
  2.8 68.9 %shard_map.46 = f32[64,32,512]{2,1,0:T(8,128)S(1)} custom-call(f32[32,64,512]{2,1,0:T(8,128)} %rhs_hbm.1, f32[64,512]{1,0:T(8,128)S(1)} %copy-done.1, f32[2,64,512]{2,1,0:T(8,128)S(1)} %copy-done, s32[64,512]{1,0:T(8,128)S(1)} %copy-done.2), custom_call_target="tpu_custom_call" | custom-call | tf_op jit(solution)/shard_map/pallas_call | solution.py:395
  71.7 4.4 %copy.5 = f32[32,64,512]{2,1,0:T(8,128)} copy(f32[32,64,512]{2,0,1:T(8,128)S(1)} %bitcast.1) | data formatting | bytes 8388608 | tf_op jit(solution)/shard_map/transpose | solution.py:429
Async XLA Ops:
  0.0 0.9 %copy-start = (f32[2,64,512]{2,1,0:T(8,128)S(1)}, f32[2,64,512]{2,1,0:T(8,128)}, u32[]{:S(2)}) copy-start(f32[2,64,512]{2,1,0:T(8,128)} %face_ref.1) | copy-start | bytes 786436
  1.0 0.9 %copy-start.1 = (f32[64,512]{1,0:T(8,128)S(1)}, f32[64,512]{1,0:T(8,128)}, u32[]{:S(2)}) copy-start(f32[64,512]{1,0:T(8,128)} %diag_ref.1) | copy-start | bytes 393220
  1.9 0.9 %copy-start.2 = (s32[64,512]{1,0:T(8,128)S(1)}, s32[64,512]{1,0:T(8,128)}, u32[]{:S(2)}) copy-start(s32[64,512]{1,0:T(8,128)} %agg_ref.1) | copy-start | bytes 393220
